TPU v7x, 128 devices: a whole 4x4x4 slice. The times are simulated.
128 devices in a mesh: gz: 4 (over z), gx: 4 (over y_lo, core), gy: 8 (over x, y_hi).
Axes of the slice: x: 4, y: 4 (y_hi: 2, y_lo: 2; y = y_hi * 2 + y_lo), z: 4, core: 2. Of those that a mesh axis runs over, the one named last changes fastest.
Arguments:
- right_side: float32 [40, 128, 6, 1024], P('gz', 'gy', None, 'gx'), may hold values from -0.0625 to 0.0625
- previous: float32 [40, 128, 6, 1024], P('gz', 'gy', None, 'gx'), may hold values from -0.15625 to 0.15625
- diag_inverse: bfloat16 [40, 128, 6, 6, 1024], P('gz', 'gy', None, None, 'gx'), may hold values from -0.6 to 2.6, as said below
- jacobians: bfloat16 [40, 128, 6, 6, 6, 1024], P('gz', 'gy', None, None, None, 'gx'), may hold values from -3 to 3, as said below
Outputs:
- update: float32 [40, 128, 6, 1024], P('gz', 'gy', None, 'gx')
Inputs may be any that keep to these rules, and one draw needn't show every extreme that they name: `diag_inverse`: entries of the cells' inverted diagonal blocks. `jacobians`: entries of the cells' coupling blocks.
All inputs are finite; a program needn't handle non-finite values.
Results may differ from a plain program's by a relative error of at most 0.0003.
Values sent between devices are 32-bit elements; how exact they have to be, the bound alone decides.
A program may use at most 128 MiB of HBM per device.

v0:
```python
import jax
import jax.numpy as jnp
from jax import lax
from jax.sharding import PartitionSpec as P


def extended(x, sides, width):
    for axis, dim in sides:
        devices, length = (lax.axis_size(axis), x.shape[dim])
        up = [(i, (i + 1) % devices) for i in range(devices - 1)]
        down = [(j, i) for i, j in up]
        last = lax.slice_in_dim(x, length - width, length, axis=dim)
        initial = lax.slice_in_dim(x, 0, width, axis=dim)
        before = lax.ppermute(last, axis, up)
        after = lax.ppermute(initial, axis, down)
        x = jnp.concatenate([before, x, after], axis=dim)
    return x


def shifted(x, axis, by):
    devices = lax.axis_size(axis)
    pairs = [(i, i + by) for i in range(devices) if 0 <= i + by < devices]
    return lax.ppermute(x, axis, pairs)


def block_apply(blocks, vector):
    return jnp.sum(blocks * vector[..., None, :, :], axis=-2)


def slab_inplane(jacobians, padded):
    total = block_apply(jacobians[:, :, 0].astype(jnp.float32), padded[:, 1:-1, :, :-2])
    total = total + block_apply(jacobians[:, :, 1].astype(jnp.float32), padded[:, 1:-1, :, 2:])
    total = total + block_apply(jacobians[:, :, 2].astype(jnp.float32), padded[:, :-2, :, 1:-1])
    total = total + block_apply(jacobians[:, :, 3].astype(jnp.float32), padded[:, 2:, :, 1:-1])
    return total


def body(right_side, previous, diag_inverse, jacobians):
    planes_y = right_side.shape[1]
    planes_x = right_side.shape[3]
    zeros_plane = jnp.zeros((planes_y, 6, planes_x), jnp.float32)
    inverse_all = diag_inverse.astype(jnp.float32)
    lower_all = jacobians[:, :, 4].astype(jnp.float32)
    upper_all = jacobians[:, :, 5].astype(jnp.float32)
    padded_old = extended(previous, (("gx", 3), ("gy", 1)), 1)
    source_all = right_side - slab_inplane(jacobians, padded_old)

    def forward_sweep(incoming):

        def forward_step(earlier, planes):
            source, inverse, lower = planes
            result = block_apply(inverse, source - block_apply(lower, earlier))
            return (result, result)

        return lax.scan(forward_step, incoming, (source_all, inverse_all, lower_all), unroll=True)

    incoming = zeros_plane
    for handoff_step in range(lax.axis_size("gz") - 1):
        final_plane, sweep_values = forward_sweep(incoming)
        incoming = shifted(final_plane, "gz", 1)
    final_plane, sweep_values = forward_sweep(incoming)
    padded_new = extended(sweep_values - previous, (("gx", 3), ("gy", 1)), 1)
    inner_all = slab_inplane(jacobians, padded_new)

    def backward_sweep(incoming):

        def backward_step(later, planes):
            forward_plane, inner, inverse, upper = planes
            change = block_apply(upper, later) + inner
            result = forward_plane - block_apply(inverse, change)
            return (result, result)

        return lax.scan(
            backward_step,
            incoming,
            (sweep_values, inner_all, inverse_all, upper_all),
            reverse=True,
            unroll=True,
        )

    incoming = zeros_plane
    for handoff_step in range(lax.axis_size("gz") - 1):
        bottom_plane, update = backward_sweep(incoming)
        incoming = shifted(bottom_plane, "gz", -1)
    bottom_plane, update = backward_sweep(incoming)
    return update


def solution(mesh):
    placed = (
        P("gz", "gy", None, "gx"),
        P("gz", "gy", None, "gx"),
        P("gz", "gy", None, None, "gx"),
        P("gz", "gy", None, None, None, "gx"),
    )
    return jax.shard_map(
        body, mesh=mesh, in_specs=placed, out_specs=P("gz", "gy", None, "gx"), check_vma=False
    )
```

profile of v0, /device:TPU:74, one launch (start us, length us, event | category | flops | bytes accessed | tf_op | source)
XLA Modules:
  0.0 138.0 jit_solution(16919533047008321821)
XLA Ops:
  4.4 2.7 %collective-permute-start = (f32[10,16,6,1]{1,2,3,0:T(8,128)S(1)}, f32[10,16,6,1]{1,2,3,0:T(8,128)S(1)}, u32[]{:S(2)}, u32[]{:S(2)}) collective-permute-start(f32[10,16,6,1]{1,2,3,0:T(8,128)S(1)} %copy.21), channel_id=1, source_target_pairs={{0,8},{8,16},{16,24},{1,9},{9,17},{17,25},{2,10},{10,18},{18,26},{... | collective-permute-start | bytes 11528 | tf_op jit(solution)/shard_map/ppermute | solution.py:14
  7.0 6.3 %slice_convert_fusion.1 = (f32[10,16,1,6,6,256]{5,1,4,3,2,0:T(8,128)S(1)}, f32[10,16,1,6,6,256]{5,1,4,3,2,0:T(8,128)}) fusion(bf16[10,16,6,6,6,256]{5,1,4,3,2,0:T(8,128)(2,1)} %param.7), kind=kLoop, calls=%fused_computation.17 | loop fusion | flops 2949120 | bytes 17694720 | tf_op jit(solution)/shard_map/convert_element_type | solution.py:43
  14.1 3.6 %convert_element_type.39 = f32[10,16,6,6,256]{4,1,3,2,0:T(8,128)} convert(bf16[10,16,6,6,256]{4,1,3,2,0:T(8,128)(2,1)S(1)} %copy-done.2) | non-fusion elementwise | flops 1474560 | bytes 8847360 | tf_op jit(solution)/shard_map/convert_element_type | solution.py:42
  21.3 4.2 %collective-permute-start.2 = (f32[10,1,6,258]{3,2,1,0:T(8,128)}, f32[10,1,6,258]{3,2,1,0:T(8,128)}, u32[]{:S(2)}, u32[]{:S(2)}) collective-permute-start(f32[10,1,6,258]{3,2,1,0:T(8,128)} %get-tuple-element.17), channel_id=1, source_target_pairs={{0,1},{1,2},{2,3},{3,4},{4,5},{5,6},{6,7},{8,9},{9,10},{10,11},{11... | collective-permute-start | bytes 185768 | tf_op jit(solution)/shard_map/ppermute | solution.py:14
  25.5 4.0 %collective-permute-start.3 = (f32[10,1,6,258]{3,2,1,0:T(8,128)}, f32[10,1,6,258]{3,2,1,0:T(8,128)}, u32[]{:S(2)}, u32[]{:S(2)}) collective-permute-start(f32[10,1,6,258]{3,2,1,0:T(8,128)} %get-tuple-element.18), channel_id=1, source_target_pairs={{1,0},{2,1},{3,2},{4,3},{5,4},{6,5},{7,6},{9,8},{10,9},{11,10},{12... | collective-permute-start | bytes 185768 | tf_op jit(solution)/shard_map/ppermute | solution.py:15
  37.0 7.6 %fusion.2 = (f32[10,16,6,256]{3,1,2,0:T(8,128)S(1)}, f32[10,16,6,256]{3,1,2,0:T(8,128)S(1)}, f32[10,16,6,256]{3,1,2,0:T(8,128)S(1)}, f32[10,16,6,256]{3,1,2,0:T(8,128)S(1)}) fusion(f32[10,16,6,256]{3,1,2,0:T(8,128)S(1)} %get-tuple-element.28, bf16[10,16,6,6,6,256]{5,1,4,3,2,0:T(8,128)(2,1)} %param.7, f32[10,16,6,256]{3,1,2,0:T(8,128)S(1)} %copy.20, ...), kind=kLoop, calls=%fused_computation.10 | loop fusion | flops 16711680 | bytes 19660800 | tf_op jit(solution)/shard_map/reduce_sum | solution.py:27
  46.8 3.7 %collective-permute-start.4 = (f32[16,6,256]{2,0,1:T(8,128)S(1)}, f32[16,6,256]{2,0,1:T(8,128)S(1)}, u32[]{:S(2)}, u32[]{:S(2)}) collective-permute-start(f32[16,6,256]{2,0,1:T(8,128)S(1)} %multiply_reduce_fusion.140), channel_id=1, source_target_pairs={{0,32},{32,64},{64,96},{1,33},{33,65},{65,97},{2,34},{34,66},{66,9... | collective-permute-start | bytes 294920 | tf_op jit(solution)/shard_map/ppermute | solution.py:23
  50.5 2.8 %collective-permute-done.4 = f32[16,6,256]{2,0,1:T(8,128)S(1)} collective-permute-done((f32[16,6,256]{2,0,1:T(8,128)S(1)}, f32[16,6,256]{2,0,1:T(8,128)S(1)}, u32[]{:S(2)}, u32[]{:S(2)}) %collective-permute-start.4) | collective-permute-done | bytes 98336 | tf_op jit(solution)/shard_map/ppermute | solution.py:23
  54.9 3.5 %collective-permute-start.5 = (f32[16,6,256]{2,0,1:T(8,128)S(1)}, f32[16,6,256]{2,0,1:T(8,128)S(1)}, u32[]{:S(2)}, u32[]{:S(2)}) collective-permute-start(f32[16,6,256]{2,0,1:T(8,128)S(1)} %multiply_reduce_fusion.120), channel_id=1, source_target_pairs={{0,32},{32,64},{64,96},{1,33},{33,65},{65,97},{2,34},{34,66},{66,9... | collective-permute-start | bytes 294920 | tf_op jit(solution)/shard_map/ppermute | solution.py:23
  58.5 3.0 %collective-permute-done.5 = f32[16,6,256]{2,0,1:T(8,128)S(1)} collective-permute-done((f32[16,6,256]{2,0,1:T(8,128)S(1)}, f32[16,6,256]{2,0,1:T(8,128)S(1)}, u32[]{:S(2)}, u32[]{:S(2)}) %collective-permute-start.5) | collective-permute-done | bytes 98336 | tf_op jit(solution)/shard_map/ppermute | solution.py:23
  63.0 3.5 %collective-permute-start.6 = (f32[16,6,256]{2,0,1:T(8,128)S(1)}, f32[16,6,256]{2,0,1:T(8,128)S(1)}, u32[]{:S(2)}, u32[]{:S(2)}) collective-permute-start(f32[16,6,256]{2,0,1:T(8,128)S(1)} %multiply_reduce_fusion.100), channel_id=1, source_target_pairs={{0,32},{32,64},{64,96},{1,33},{33,65},{65,97},{2,34},{34,66},{66,9... | collective-permute-start | bytes 294920 | tf_op jit(solution)/shard_map/ppermute | solution.py:23
  66.6 3.0 %collective-permute-done.6 = f32[16,6,256]{2,0,1:T(8,128)S(1)} collective-permute-done((f32[16,6,256]{2,0,1:T(8,128)S(1)}, f32[16,6,256]{2,0,1:T(8,128)S(1)}, u32[]{:S(2)}, u32[]{:S(2)}) %collective-permute-start.6) | collective-permute-done | bytes 98336 | tf_op jit(solution)/shard_map/ppermute | solution.py:23
  75.3 3.6 %collective-permute-start.8 = (f32[10,16,6,1]{3,1,2,0:T(8,128)S(1)}, f32[10,16,6,1]{3,1,2,0:T(8,128)S(1)}, u32[]{:S(2)}, u32[]{:S(2)}) collective-permute-start(f32[10,16,6,1]{3,1,2,0:T(8,128)S(1)} %get-tuple-element.26), channel_id=1, source_target_pairs={{8,0},{16,8},{24,16},{9,1},{17,9},{25,17},{10,2},{18,10},{26,18},{... | collective-permute-start | bytes 11528 | tf_op jit(solution)/shard_map/ppermute | solution.py:15
  78.9 4.6 %collective-permute-done.7 = f32[10,16,6,1]{3,1,2,0:T(8,128)S(1)} collective-permute-done((f32[10,16,6,1]{3,1,2,0:T(8,128)S(1)}, f32[10,16,6,1]{3,1,2,0:T(8,128)S(1)}, u32[]{:S(2)}, u32[]{:S(2)}) %collective-permute-start.7) | collective-permute-done | bytes 3872 | tf_op jit(solution)/shard_map/ppermute | solution.py:14
  85.8 5.5 %collective-permute-start.10 = (f32[10,1,6,258]{3,1,2,0:T(1,128)S(1)}, f32[10,1,6,258]{3,1,2,0:T(1,128)S(1)}, u32[]{:S(2)}, u32[]{:S(2)}) collective-permute-start(f32[10,1,6,258]{3,1,2,0:T(1,128)S(1)} %get-tuple-element.21), channel_id=1, source_target_pairs={{1,0},{2,1},{3,2},{4,3},{5,4},{6,5},{7,6},{9,8},{10,9},{11,10},{12... | collective-permute-start | bytes 185768 | tf_op jit(solution)/shard_map/ppermute | solution.py:15
  91.4 2.2 %collective-permute-start.9 = (f32[10,1,6,258]{3,1,2,0:T(1,128)S(1)}, f32[10,1,6,258]{3,1,2,0:T(1,128)S(1)}, u32[]{:S(2)}, u32[]{:S(2)}) collective-permute-start(f32[10,1,6,258]{3,1,2,0:T(1,128)S(1)} %get-tuple-element.22), channel_id=1, source_target_pairs={{0,1},{1,2},{2,3},{3,4},{4,5},{5,6},{6,7},{8,9},{9,10},{10,11},{11... | collective-permute-start | bytes 185768 | tf_op jit(solution)/shard_map/ppermute | solution.py:14
  93.9 6.3 %collective-permute-done.9 = f32[10,1,6,258]{3,1,2,0:T(1,128)S(1)} collective-permute-done((f32[10,1,6,258]{3,1,2,0:T(1,128)S(1)}, f32[10,1,6,258]{3,1,2,0:T(1,128)S(1)}, u32[]{:S(2)}, u32[]{:S(2)}) %collective-permute-start.9) | collective-permute-done | bytes 61952 | tf_op jit(solution)/shard_map/ppermute | solution.py:14
  101.5 7.4 %fusion.3 = (f32[10,16,6,256]{3,1,2,0:T(8,128)S(1)}, f32[10,16,6,256]{3,1,2,0:T(8,128)S(1)}, f32[10,16,6,256]{3,1,2,0:T(8,128)S(1)}, f32[10,16,6,256]{3,1,2,0:T(8,128)S(1)}) fusion(f32[10,16,6,256]{3,1,2,0:T(8,128)S(1)} %get-tuple-element.24, bf16[10,16,6,6,6,256]{5,1,4,3,2,0:T(8,128)(2,1)} %param.7, f32[10,16,6,256]{3,1,2,0:T(8,128)S(1)} %get-tuple-element.23, ...), kind=kLoop, calls=%fused_computation.11 | loop fusion | flops 16711680 | bytes 19660800 | tf_op jit(solution)/shard_map/reduce_sum | solution.py:27
  111.2 2.0 %collective-permute-start.11 = (f32[16,6,256]{2,0,1:T(8,128)S(1)}, f32[16,6,256]{2,0,1:T(8,128)S(1)}, u32[]{:S(2)}, u32[]{:S(2)}) collective-permute-start(f32[16,6,256]{2,0,1:T(8,128)S(1)} %sub.689), channel_id=1, source_target_pairs={{32,0},{64,32},{96,64},{33,1},{65,33},{97,65},{34,2},{66,34},{98,6... | collective-permute-start | bytes 294920 | tf_op jit(solution)/shard_map/ppermute | solution.py:23
  113.2 4.5 %collective-permute-done.11 = f32[16,6,256]{2,0,1:T(8,128)S(1)} collective-permute-done((f32[16,6,256]{2,0,1:T(8,128)S(1)}, f32[16,6,256]{2,0,1:T(8,128)S(1)}, u32[]{:S(2)}, u32[]{:S(2)}) %collective-permute-start.11) | collective-permute-done | bytes 98336 | tf_op jit(solution)/shard_map/ppermute | solution.py:23
  119.5 2.0 %collective-permute-start.12 = (f32[16,6,256]{2,0,1:T(8,128)S(1)}, f32[16,6,256]{2,0,1:T(8,128)S(1)}, u32[]{:S(2)}, u32[]{:S(2)}) collective-permute-start(f32[16,6,256]{2,0,1:T(8,128)S(1)} %sub.699), channel_id=1, source_target_pairs={{32,0},{64,32},{96,64},{33,1},{65,33},{97,65},{34,2},{66,34},{98,6... | collective-permute-start | bytes 294920 | tf_op jit(solution)/shard_map/ppermute | solution.py:23
  121.6 4.5 %collective-permute-done.12 = f32[16,6,256]{2,0,1:T(8,128)S(1)} collective-permute-done((f32[16,6,256]{2,0,1:T(8,128)S(1)}, f32[16,6,256]{2,0,1:T(8,128)S(1)}, u32[]{:S(2)}, u32[]{:S(2)}) %collective-permute-start.12) | collective-permute-done | bytes 98336 | tf_op jit(solution)/shard_map/ppermute | solution.py:23
  127.9 2.0 %collective-permute-start.13 = (f32[16,6,256]{2,0,1:T(8,128)S(1)}, f32[16,6,256]{2,0,1:T(8,128)S(1)}, u32[]{:S(2)}, u32[]{:S(2)}) collective-permute-start(f32[16,6,256]{2,0,1:T(8,128)S(1)} %sub.709), channel_id=1, source_target_pairs={{32,0},{64,32},{96,64},{33,1},{65,33},{97,65},{34,2},{66,34},{98,6... | collective-permute-start | bytes 294920 | tf_op jit(solution)/shard_map/ppermute | solution.py:23
  129.9 4.5 %collective-permute-done.13 = f32[16,6,256]{2,0,1:T(8,128)S(1)} collective-permute-done((f32[16,6,256]{2,0,1:T(8,128)S(1)}, f32[16,6,256]{2,0,1:T(8,128)S(1)}, u32[]{:S(2)}, u32[]{:S(2)}) %collective-permute-start.13) | collective-permute-done | bytes 98336 | tf_op jit(solution)/shard_map/ppermute | solution.py:23
  (354 shorter events, 38.4 us)
Async XLA Ops:
  1.9 15.8 %collective-permute-start.1 = (f32[10,16,6,1]{1,2,3,0:T(8,128)S(1)}, f32[10,16,6,1]{1,2,3,0:T(8,128)S(1)}, u32[]{:S(2)}, u32[]{:S(2)}) collective-permute-start(f32[10,16,6,1]{1,2,3,0:T(8,128)S(1)} %copy.22), channel_id=1, source_target_pairs={{8,0},{16,8},{24,16},{9,1},{17,9},{25,17},{10,2},{18,10},{26,18},{... | collective-permute-start | bytes 11528 | tf_op jit(solution)/shard_map/ppermute | solution.py:15
  4.4 9.1 %copy-start.1 = (f32[10,16,6,256]{3,1,2,0:T(8,128)S(1)}, f32[10,16,6,256]{3,1,2,0:T(8,128)}, u32[]{:S(2)}) copy-start(f32[10,16,6,256]{3,1,2,0:T(8,128)} %param.5) | copy-start | bytes 2949124
  4.4 9.7 %copy-start.2 = (bf16[10,16,6,6,256]{4,1,3,2,0:T(8,128)(2,1)S(1)}, bf16[10,16,6,6,256]{4,1,3,2,0:T(8,128)(2,1)}, u32[]{:S(2)}) copy-start(bf16[10,16,6,6,256]{4,1,3,2,0:T(8,128)(2,1)} %param.6) | copy-start | bytes 8847364
  4.4 13.9 %collective-permute-start = (f32[10,16,6,1]{1,2,3,0:T(8,128)S(1)}, f32[10,16,6,1]{1,2,3,0:T(8,128)S(1)}, u32[]{:S(2)}, u32[]{:S(2)}) collective-permute-start(f32[10,16,6,1]{1,2,3,0:T(8,128)S(1)} %copy.21), channel_id=1, source_target_pairs={{0,8},{8,16},{16,24},{1,9},{9,17},{17,25},{2,10},{10,18},{18,26},{... | collective-permute-start | bytes 11528 | tf_op jit(solution)/shard_map/ppermute | solution.py:14
  13.4 4.3 %copy-start = (f32[10,16,1,6,6,256]{5,1,4,3,2,0:T(8,128)}, f32[10,16,1,6,6,256]{5,1,4,3,2,0:T(8,128)S(1)}, u32[]{:S(2)}) copy-start(f32[10,16,1,6,6,256]{5,1,4,3,2,0:T(8,128)S(1)} %get-tuple-element.13) | copy-start | bytes 17694724
  17.7 7.8 %copy-start.4 = (f32[10,16,6,1]{1,2,3,0:T(8,128)}, f32[10,16,6,1]{1,2,3,0:T(8,128)S(1)}, u32[]{:S(2)}) copy-start(f32[10,16,6,1]{1,2,3,0:T(8,128)S(1)} %collective-permute-done.1) | copy-start | bytes 11524
  18.2 7.2 %copy-start.5 = (f32[10,16,6,1]{1,2,3,0:T(8,128)}, f32[10,16,6,1]{1,2,3,0:T(8,128)S(1)}, u32[]{:S(2)}) copy-start(f32[10,16,6,1]{1,2,3,0:T(8,128)S(1)} %collective-permute-done) | copy-start | bytes 11524
  21.3 13.2 %collective-permute-start.2 = (f32[10,1,6,258]{3,2,1,0:T(8,128)}, f32[10,1,6,258]{3,2,1,0:T(8,128)}, u32[]{:S(2)}, u32[]{:S(2)}) collective-permute-start(f32[10,1,6,258]{3,2,1,0:T(8,128)} %get-tuple-element.17), channel_id=1, source_target_pairs={{0,1},{1,2},{2,3},{3,4},{4,5},{5,6},{6,7},{8,9},{9,10},{10,11},{11... | collective-permute-start | bytes 185768 | tf_op jit(solution)/shard_map/ppermute | solution.py:14
  25.5 9.0 %collective-permute-start.3 = (f32[10,1,6,258]{3,2,1,0:T(8,128)}, f32[10,1,6,258]{3,2,1,0:T(8,128)}, u32[]{:S(2)}, u32[]{:S(2)}) collective-permute-start(f32[10,1,6,258]{3,2,1,0:T(8,128)} %get-tuple-element.18), channel_id=1, source_target_pairs={{1,0},{2,1},{3,2},{4,3},{5,4},{6,5},{7,6},{9,8},{10,9},{11,10},{12... | collective-permute-start | bytes 185768 | tf_op jit(solution)/shard_map/ppermute | solution.py:15
  37.0 8.3 %slice-start = ((s8[5898240]{0:T(1024)(128)(4,1)}), s8[4194304]{0:T(1024)(128)(4,1)S(1)}, s32[]{:S(2)}) async-start(s8[5898240]{0:T(1024)(128)(4,1)} %bitcast.666), calls=%async_computation | async-start | bytes 8388608
  37.0 8.3 %slice-start.4 = ((s8[5898240]{0:T(1024)(128)(4,1)}), s8[4194304]{0:T(1024)(128)(4,1)S(1)}, s32[]{:S(2)}) async-start(s8[5898240]{0:T(1024)(128)(4,1)} %bitcast.670), calls=%async_computation.4 | async-start | bytes 8388608
  37.0 7.6 %copy-start.3 = (f32[10,16,6,256]{3,1,2,0:T(8,128)S(1)}, f32[10,16,6,256]{3,1,2,0:T(8,128)}, u32[]{:S(2)}) copy-start(f32[10,16,6,256]{3,1,2,0:T(8,128)} %param.4) | copy-start | bytes 2949124
  37.0 8.2 %slice-start.1 = ((s8[5898240]{0:T(1024)(128)(4,1)}), s8[1703936]{0:T(1024)(128)(4,1)S(1)}, s32[]{:S(2)}) async-start(s8[5898240]{0:T(1024)(128)(4,1)} %bitcast.666), calls=%async_computation.1 | async-start | bytes 3407872
  37.0 8.3 %slice-start.5 = ((s8[5898240]{0:T(1024)(128)(4,1)}), s8[1703936]{0:T(1024)(128)(4,1)S(1)}, s32[]{:S(2)}) async-start(s8[5898240]{0:T(1024)(128)(4,1)} %bitcast.670), calls=%async_computation.5 | async-start | bytes 3407872
  46.8 6.5 %collective-permute-start.4 = (f32[16,6,256]{2,0,1:T(8,128)S(1)}, f32[16,6,256]{2,0,1:T(8,128)S(1)}, u32[]{:S(2)}, u32[]{:S(2)}) collective-permute-start(f32[16,6,256]{2,0,1:T(8,128)S(1)} %multiply_reduce_fusion.140), channel_id=1, source_target_pairs={{0,32},{32,64},{64,96},{1,33},{33,65},{65,97},{2,34},{34,66},{66,9... | collective-permute-start | bytes 294920 | tf_op jit(solution)/shard_map/ppermute | solution.py:23
  54.9 6.5 %collective-permute-start.5 = (f32[16,6,256]{2,0,1:T(8,128)S(1)}, f32[16,6,256]{2,0,1:T(8,128)S(1)}, u32[]{:S(2)}, u32[]{:S(2)}) collective-permute-start(f32[16,6,256]{2,0,1:T(8,128)S(1)} %multiply_reduce_fusion.120), channel_id=1, source_target_pairs={{0,32},{32,64},{64,96},{1,33},{33,65},{65,97},{2,34},{34,66},{66,9... | collective-permute-start | bytes 294920 | tf_op jit(solution)/shard_map/ppermute | solution.py:23
  63.0 6.5 %collective-permute-start.6 = (f32[16,6,256]{2,0,1:T(8,128)S(1)}, f32[16,6,256]{2,0,1:T(8,128)S(1)}, u32[]{:S(2)}, u32[]{:S(2)}) collective-permute-start(f32[16,6,256]{2,0,1:T(8,128)S(1)} %multiply_reduce_fusion.100), channel_id=1, source_target_pairs={{0,32},{32,64},{64,96},{1,33},{33,65},{65,97},{2,34},{34,66},{66,9... | collective-permute-start | bytes 294920 | tf_op jit(solution)/shard_map/ppermute | solution.py:23
  73.4 10.1 %collective-permute-start.7 = (f32[10,16,6,1]{3,1,2,0:T(8,128)S(1)}, f32[10,16,6,1]{3,1,2,0:T(8,128)S(1)}, u32[]{:S(2)}, u32[]{:S(2)}) collective-permute-start(f32[10,16,6,1]{3,1,2,0:T(8,128)S(1)} %get-tuple-element.25), channel_id=1, source_target_pairs={{0,8},{8,16},{16,24},{1,9},{9,17},{17,25},{2,10},{10,18},{18,26},{... | collective-permute-start | bytes 11528 | tf_op jit(solution)/shard_map/ppermute | solution.py:14
  75.3 10.0 %collective-permute-start.8 = (f32[10,16,6,1]{3,1,2,0:T(8,128)S(1)}, f32[10,16,6,1]{3,1,2,0:T(8,128)S(1)}, u32[]{:S(2)}, u32[]{:S(2)}) collective-permute-start(f32[10,16,6,1]{3,1,2,0:T(8,128)S(1)} %get-tuple-element.26), channel_id=1, source_target_pairs={{8,0},{16,8},{24,16},{9,1},{17,9},{25,17},{10,2},{18,10},{26,18},{... | collective-permute-start | bytes 11528 | tf_op jit(solution)/shard_map/ppermute | solution.py:15
  85.8 8.1 %collective-permute-start.10 = (f32[10,1,6,258]{3,1,2,0:T(1,128)S(1)}, f32[10,1,6,258]{3,1,2,0:T(1,128)S(1)}, u32[]{:S(2)}, u32[]{:S(2)}) collective-permute-start(f32[10,1,6,258]{3,1,2,0:T(1,128)S(1)} %get-tuple-element.21), channel_id=1, source_target_pairs={{1,0},{2,1},{3,2},{4,3},{5,4},{6,5},{7,6},{9,8},{10,9},{11,10},{12... | collective-permute-start | bytes 185768 | tf_op jit(solution)/shard_map/ppermute | solution.py:15
  91.4 8.8 %collective-permute-start.9 = (f32[10,1,6,258]{3,1,2,0:T(1,128)S(1)}, f32[10,1,6,258]{3,1,2,0:T(1,128)S(1)}, u32[]{:S(2)}, u32[]{:S(2)}) collective-permute-start(f32[10,1,6,258]{3,1,2,0:T(1,128)S(1)} %get-tuple-element.22), channel_id=1, source_target_pairs={{0,1},{1,2},{2,3},{3,4},{4,5},{5,6},{6,7},{8,9},{9,10},{10,11},{11... | collective-permute-start | bytes 185768 | tf_op jit(solution)/shard_map/ppermute | solution.py:14
  111.2 6.5 %collective-permute-start.11 = (f32[16,6,256]{2,0,1:T(8,128)S(1)}, f32[16,6,256]{2,0,1:T(8,128)S(1)}, u32[]{:S(2)}, u32[]{:S(2)}) collective-permute-start(f32[16,6,256]{2,0,1:T(8,128)S(1)} %sub.689), channel_id=1, source_target_pairs={{32,0},{64,32},{96,64},{33,1},{65,33},{97,65},{34,2},{66,34},{98,6... | collective-permute-start | bytes 294920 | tf_op jit(solution)/shard_map/ppermute | solution.py:23
  119.5 6.5 %collective-permute-start.12 = (f32[16,6,256]{2,0,1:T(8,128)S(1)}, f32[16,6,256]{2,0,1:T(8,128)S(1)}, u32[]{:S(2)}, u32[]{:S(2)}) collective-permute-start(f32[16,6,256]{2,0,1:T(8,128)S(1)} %sub.699), channel_id=1, source_target_pairs={{32,0},{64,32},{96,64},{33,1},{65,33},{97,65},{34,2},{66,34},{98,6... | collective-permute-start | bytes 294920 | tf_op jit(solution)/shard_map/ppermute | solution.py:23
  127.9 6.5 %collective-permute-start.13 = (f32[16,6,256]{2,0,1:T(8,128)S(1)}, f32[16,6,256]{2,0,1:T(8,128)S(1)}, u32[]{:S(2)}, u32[]{:S(2)}) collective-permute-start(f32[16,6,256]{2,0,1:T(8,128)S(1)} %sub.709), channel_id=1, source_target_pairs={{32,0},{64,32},{96,64},{33,1},{65,33},{97,65},{34,2},{66,34},{98,6... | collective-permute-start | bytes 294920 | tf_op jit(solution)/shard_map/ppermute | solution.py:23
  (3 other events, 5.4 us)
where the time goes:
time: 139 us; the launch traced here: 138 us
  other arithmetic  45.8 us (33%)
  starting transfers between devices  42.9 us (31%)
  waiting for transfers between devices  35.2 us (25%)
  local copies, waits for them, and re-layouts  11.5 us (8%)
  between operations  2.55 us (2%)
    reduce_sum x161, other arithmetic, block_apply(): return jnp.sum(blocks * vector[..., None, :, :], axis=-2)  24.8 us
    ppermute x6, waiting for transfers between devices, shifted(): return lax.ppermute(x, axis, pairs)  22.2 us
    ppermute x6, starting transfers between devices, shifted(): return lax.ppermute(x, axis, pairs)  16.8 us
    ppermute x4, starting transfers between devices, extended(): after = lax.ppermute(initial, axis, down)  15.2 us
    ppermute x4, starting transfers between devices, extended(): before = lax.ppermute(last, axis, up)  11 us
    ppermute x4, waiting for transfers between devices, extended(): before = lax.ppermute(last, axis, up)  10.9 us
    convert_element_type x1, other arithmetic, body(): lower_all = jacobians[:, :, 4].astype(jnp.float32)  6.34 us
    concatenate x4, other arithmetic, extended(): x = jnp.concatenate([before, x, after], axis=dim)  5.4 us
  transfers between devices with their start and end apart: 14, of which 10 were waited for; matrix products, arithmetic and copies ran while one was open for 12% of the time, Pallas kernels for 0%

commit v1 on v0

v1 whole, which is shorter than its diff:
```python
import functools

import jax
import jax.numpy as jnp
from jax import lax
from jax.experimental import pallas as pl
from jax.experimental.pallas import tpu as pltpu
from jax.sharding import PartitionSpec as P

F32 = jnp.float32
V = 6
TILE_Y, TILE_X = 8, 128
CHUNKS = ((0, 0), (1, 0), (0, 1), (1, 1))


def kernel(sizes, rhs_h, prev_h, dinv_h, jac_h, out_ref, jv, dv, rv, pv, sv,
           send_y, recv_y, send_x, recv_x, send_z, recv_z,
           ld_p, ld_r, ld_j, ld_l, ld_d, ld_u, ssy, rsy, ssx, rsx, ssz, rsz):
    nz, nx, ny = sizes
    planes, _, rows, cols = rhs_h.shape
    iz, ix, iy = (lax.axis_index(a) for a in ("gz", "gx", "gy"))

    load_prev = pltpu.make_async_copy(prev_h, pv, ld_p)
    load_prev.start()

    def load_first(z):
        return (
            pltpu.make_async_copy(jac_h.at[z, pl.ds(0, 4)], jv.at[z, pl.ds(0, 4)], ld_j.at[z]),
            pltpu.make_async_copy(rhs_h.at[z], rv.at[z], ld_r.at[z]),
        )

    def load_lower(z):
        return (
            pltpu.make_async_copy(jac_h.at[z, 4], jv.at[z, 4], ld_l.at[z]),
            pltpu.make_async_copy(dinv_h.at[z], dv.at[z], ld_d.at[z]),
        )

    def load_upper(z):
        return (pltpu.make_async_copy(jac_h.at[z, 5], jv.at[z, 5], ld_u.at[z]),)

    for group in (load_first, load_lower, load_upper):

        @pl.loop(0, planes)
        def _(z):
            for copy in group(z):
                copy.start()

    sides = (
        ("gy", -1, iy > 0), ("gy", 1, iy < ny - 1),
        ("gx", -1, ix > 0), ("gx", 1, ix < nx - 1),
        ("gz", -1, iz > 0), ("gz", 1, iz < nz - 1),
    )
    at = {"gz": iz, "gx": ix, "gy": iy}
    barrier = pltpu.get_barrier_semaphore()
    for axis, step, exists in sides:

        @pl.when(exists)
        def _():
            pl.semaphore_signal(
                barrier, inc=1, device_id={axis: at[axis] + step},
                device_id_type=pl.DeviceIdType.MESH)

    def copy_y(e, yh, xh):
        step = 2 * yh - 1
        return pltpu.make_async_remote_copy(
            send_y.at[e, yh, xh], recv_y.at[e, 1 - yh, xh], ssy.at[e, yh, xh],
            rsy.at[e, 1 - yh, xh], device_id={"gy": iy + step},
            device_id_type=pl.DeviceIdType.MESH)

    def copy_x(e, yh, xh):
        step = 2 * xh - 1
        return pltpu.make_async_remote_copy(
            send_x.at[e, xh, yh], recv_x.at[e, 1 - xh, yh], ssx.at[e, xh, yh],
            rsx.at[e, 1 - xh, yh], device_id={"gx": ix + step},
            device_id_type=pl.DeviceIdType.MESH)

    def copy_z(d, c):
        step = 1 - 2 * d
        return pltpu.make_async_remote_copy(
            send_z.at[d, c], recv_z.at[d, c], ssz.at[d, c], rsz.at[d, c],
            device_id={"gz": iz + step}, device_id_type=pl.DeviceIdType.MESH)

    has_y = (iy > 0, iy < ny - 1)
    has_x = (ix > 0, ix < nx - 1)

    def start_faces(e, yh, xh):
        @pl.when(has_y[yh])
        def _():
            copy_y(e, yh, xh).start()

        @pl.when(has_x[xh])
        def _():
            copy_x(e, yh, xh).start()

    def wait_faces(e, yh, xh):
        @pl.when(has_y[yh])
        def _():
            copy_y(e, 1 - yh, xh).wait_recv()

        @pl.when(has_x[xh])
        def _():
            copy_x(e, yh, 1 - xh).wait_recv()

    for side in range(2):

        @pl.when(jnp.logical_not(has_y[side]))
        def _():
            for e in range(2):
                for xh in range(2):
                    recv_y[e, side, xh] = jnp.zeros(recv_y.shape[3:], F32)

        @pl.when(jnp.logical_not(has_x[side]))
        def _():
            for e in range(2):
                for yh in range(2):
                    recv_x[e, side, yh] = jnp.zeros(recv_x.shape[3:], F32)

    lane8 = lax.broadcasted_iota(jnp.int32, (TILE_Y, TILE_X), 1)
    row8 = lax.broadcasted_iota(jnp.int32, (TILE_Y, TILE_X), 0)

    def cut(yh, xh):
        return pl.ds(yh * TILE_Y, TILE_Y), pl.ds(xh * TILE_X, TILE_X)

    def pack_faces(e, yh, xh, z, values, packed):
        for v in range(V):
            index = z * V + v
            edge = (TILE_Y - 1) * yh
            send_y[e, yh, xh, index] = values[v][edge:edge + 1, :]
            packed = jnp.where(
                lane8 == index, pltpu.roll(values[v], lax.rem(index + xh, TILE_X), 1), packed)
        return packed

    load_prev.wait()
    for yh, xh in CHUNKS:
        ys, xs = cut(yh, xh)

        def pack(z, packed):
            return pack_faces(0, yh, xh, z, [pv[z, v, ys, xs] for v in range(V)], packed)

        send_x[0, xh, yh] = lax.fori_loop(0, planes, pack, jnp.zeros((TILE_Y, TILE_X), F32))

    pl.semaphore_wait(barrier, sum(exists.astype(jnp.int32) for _, _, exists in sides))

    for yh, xh in CHUNKS:
        start_faces(0, yh, xh)

    lane = lax.broadcasted_iota(jnp.int32, (rows, cols), 1)
    row = lax.broadcasted_iota(jnp.int32, (rows, cols), 0)
    shifts = (
        (lane == 0, 1, 1), (lane == cols - 1, cols - 1, 1),
        (row == 0, 1, 0), (row == rows - 1, rows - 1, 0),
    )

    def interior(z, subtract):
        f = [pv[z, v] for v in range(V)]
        for n, (edge, shift, axis) in enumerate(shifts):
            g = [jnp.where(edge, 0.0, pltpu.roll(x, shift, axis)) for x in f]
            for a in range(V):
                total = jv[z, n, a, 0].astype(F32) * g[0]
                for b in range(1, V):
                    total = total + jv[z, n, a, b].astype(F32) * g[b]
                if subtract:
                    rv[z, a] = rv[z, a] - total
                elif n == 0:
                    rv[z, a] = total
                else:
                    rv[z, a] = rv[z, a] + total

    def matvec(blocks, vector):
        out = []
        for a in range(V):
            terms = [blocks(a, b).astype(F32) * vector[b] for b in range(V)]
            out.append(((terms[0] + terms[1]) + (terms[2] + terms[3])) + (terms[4] + terms[5]))
        return out

    def add_halo(e, yh, xh, sign):
        ys, xs = cut(yh, xh)
        wait_faces(e, yh, xh)
        packed = recv_x[e, xh, yh]
        on_row = row8 == (TILE_Y - 1) * yh
        on_lane = lane8 == (TILE_X - 1) * xh

        @pl.loop(0, planes)
        def _(z):
            hy, hx = [], []
            for v in range(V):
                index = z * V + v
                hy.append(jnp.where(on_row, recv_y[e, yh, xh, index], 0.0))
                turn = lax.rem(TILE_X + (TILE_X - 1) * xh - index, TILE_X)
                hx.append(jnp.where(on_lane, pltpu.roll(packed, turn, 1), 0.0))
            fx = matvec(lambda a, b: jv[z, xh, a, b, ys, xs], hx)
            fy = matvec(lambda a, b: jv[z, 2 + yh, a, b, ys, xs], hy)
            for a in range(V):
                rv[z, a, ys, xs] = rv[z, a, ys, xs] + sign * (fx[a] + fy[a])

    def sweep_up(c, incoming):
        yh, xh = CHUNKS[c]
        ys, xs = cut(yh, xh)

        def step(z, carry):
            below, packed = carry
            lower = matvec(lambda a, b: jv[z, 4, a, b, ys, xs], below)
            source = [rv[z, a, ys, xs] - lower[a] for a in range(V)]
            result = matvec(lambda a, b: dv[z, a, b, ys, xs], source)
            change = []
            for a in range(V):
                sv[z, a, ys, xs] = result[a]
                change.append(result[a] - pv[z, a, ys, xs])
                pv[z, a, ys, xs] = change[a]
            return tuple(result), pack_faces(1, yh, xh, z, change, packed)

        top, packed = lax.fori_loop(
            0, planes, step, (tuple(incoming), jnp.zeros((TILE_Y, TILE_X), F32)))
        for v in range(V):
            send_z[0, c, v] = top[v]
        send_x[1, xh, yh] = packed

        @pl.when(iz < nz - 1)
        def _():
            copy_z(0, c).start()

        start_faces(1, yh, xh)

    def sweep_down(c, incoming):
        ys, xs = cut(*CHUNKS[c])

        def step(i, above):
            z = planes - 1 - i
            upper = matvec(lambda a, b: jv[z, 5, a, b, ys, xs], above)
            change = [rv[z, a, ys, xs] + upper[a] for a in range(V)]
            change = matvec(lambda a, b: dv[z, a, b, ys, xs], change)
            result = [sv[z, a, ys, xs] - change[a] for a in range(V)]
            for a in range(V):
                out_ref[z, a, ys, xs] = result[a]
            return tuple(result)

        bottom = lax.fori_loop(0, planes, step, tuple(incoming))
        for v in range(V):
            send_z[1, c, v] = bottom[v]

        @pl.when(iz > 0)
        def _():
            copy_z(1, c).start()

    zeros = [jnp.zeros((TILE_Y, TILE_X), F32)] * V

    @pl.loop(0, planes)
    def _(z):
        for copy in load_first(z):
            copy.wait()
        interior(z, True)

    @pl.loop(0, planes)
    def _(z):
        for copy in load_lower(z):
            copy.wait()

    for c, (yh, xh) in enumerate(CHUNKS):
        add_halo(0, yh, xh, -1.0)

        @pl.when(iz == 0)
        def _():
            sweep_up(c, zeros)

    @pl.when(iz > 0)
    def _():
        for c in range(len(CHUNKS)):
            copy_z(0, c).wait_recv()
            sweep_up(c, [recv_z[0, c, v] for v in range(V)])

    @pl.loop(0, planes)
    def _(z):
        interior(z, False)

    @pl.loop(0, planes)
    def _(z):
        for copy in load_upper(z):
            copy.wait()

    for c, (yh, xh) in enumerate(CHUNKS):
        add_halo(1, yh, xh, 1.0)

        @pl.when(iz == nz - 1)
        def _():
            sweep_down(c, zeros)

    @pl.when(iz < nz - 1)
    def _():
        for c in range(len(CHUNKS)):
            copy_z(1, c).wait_recv()
            sweep_down(c, [recv_z[1, c, v] for v in range(V)])

    for e in range(2):
        for yh, xh in CHUNKS:

            @pl.when(has_y[yh])
            def _():
                copy_y(e, yh, xh).wait_send()

            @pl.when(has_x[xh])
            def _():
                copy_x(e, yh, xh).wait_send()

    for c in range(len(CHUNKS)):

        @pl.when(iz < nz - 1)
        def _():
            copy_z(0, c).wait_send()

        @pl.when(iz > 0)
        def _():
            copy_z(1, c).wait_send()


def body(sizes, right_side, previous, diag_inverse, jacobians):
    rhs = jnp.transpose(right_side, (0, 2, 1, 3))
    prev = jnp.transpose(previous, (0, 2, 1, 3))
    dinv = jnp.transpose(diag_inverse, (0, 2, 3, 1, 4))
    jac = jnp.transpose(jacobians, (0, 2, 3, 4, 1, 5))
    planes, _, rows, cols = rhs.shape
    faces = planes * V
    n = len(CHUNKS)
    hbm = pl.BlockSpec(memory_space=pl.ANY)
    dma = pltpu.SemaphoreType.DMA
    out = pl.pallas_call(
        functools.partial(kernel, sizes),
        out_shape=jax.ShapeDtypeStruct(rhs.shape, F32),
        in_specs=[hbm] * 4,
        out_specs=pl.BlockSpec(memory_space=pltpu.VMEM),
        scratch_shapes=[
            pltpu.VMEM(jac.shape, jac.dtype),
            pltpu.VMEM(dinv.shape, dinv.dtype),
            pltpu.VMEM(rhs.shape, F32),
            pltpu.VMEM(rhs.shape, F32),
            pltpu.VMEM(rhs.shape, F32),
            pltpu.VMEM((2, 2, 2, faces, 1, TILE_X), F32),
            pltpu.VMEM((2, 2, 2, faces, 1, TILE_X), F32),
            pltpu.VMEM((2, 2, 2, TILE_Y, TILE_X), F32),
            pltpu.VMEM((2, 2, 2, TILE_Y, TILE_X), F32),
            pltpu.VMEM((2, n, V, TILE_Y, TILE_X), F32),
            pltpu.VMEM((2, n, V, TILE_Y, TILE_X), F32),
            dma, dma((planes,)), dma((planes,)), dma((planes,)), dma((planes,)), dma((planes,)),
            dma((2, 2, 2)), dma((2, 2, 2)), dma((2, 2, 2)), dma((2, 2, 2)),
            dma((2, n)), dma((2, n)),
        ],
        compiler_params=pltpu.CompilerParams(
            collective_id=0, has_side_effects=True, vmem_limit_bytes=60 * 1024 * 1024),
        name="sweep_pair",
    )(rhs, prev, dinv, jac)
    return jnp.transpose(out, (0, 2, 1, 3))


def solution(mesh):
    placed = (
        P("gz", "gy", None, "gx"),
        P("gz", "gy", None, "gx"),
        P("gz", "gy", None, None, "gx"),
        P("gz", "gy", None, None, None, "gx"),
    )
    sizes = tuple(mesh.shape[a] for a in ("gz", "gx", "gy"))
    return jax.shard_map(
        functools.partial(body, sizes), mesh=mesh, in_specs=placed,
        out_specs=P("gz", "gy", None, "gx"), check_vma=False,
    )
```

time: 139 us -> 50 us (0.36)
  the two profiles are of different devices: /device:TPU:74 before, /device:TPU:6 now
where the time goes in v1:
time: 50 us; the launch traced here: 49.8 us
  Pallas kernels  47.6 us (95%)
  local copies, waits for them, and re-layouts  2.21 us (4%)
    pallas_call x1, Pallas kernels, body(): pl.pallas_call(functools.partial(kernel, sizes), out_shape=jax.ShapeDtype...  47.6 us
    unnamed x1, local copies, waits for them, and re-layouts  2.21 us

profile of v1, /device:TPU:6, one launch (start us, length us, event | category | flops | bytes accessed | tf_op | source)
XLA Modules:
  0.0 49.8 jit_solution(1040468936442984430)
XLA Ops:
  0.0 47.6 %sweep_pair.1 = f32[10,6,16,256]{3,2,1,0:T(8,128)} custom-call(f32[10,6,16,256]{3,2,1,0:T(8,128)} %bitcast.8, f32[10,6,16,256]{3,2,1,0:T(8,128)} %bitcast.9, bf16[10,6,6,16,256]{4,3,2,1,0:T(8,128)(2,1)} %bitcast.7, bf16[10,6,6,6,16,256]{5,4,3,2,1,0:T(8,128)(2,1)} %bitcast.5), custom_call_target="tpu_custom_call" | custom-call | tf_op jit(solution)/shard_map/sweep_pair/pallas_call | solution.py:325
  47.6 2.2 %copy.6 = f32[10,16,6,256]{3,1,2,0:T(8,128)} copy(f32[10,16,6,256]{3,1,2,0:T(8,128)} %bitcast.6) | data formatting | bytes 1966080

commit v2 on v1

--- a/solution.py
+++ b/solution.py
@@ -10,6 +10,7 @@
 F32 = jnp.float32
 V = 6
 TILE_Y, TILE_X = 8, 128
+PLANES_AT_ONCE = 5
 CHUNKS = ((0, 0), (1, 0), (0, 1), (1, 1))
 
 
@@ -101,6 +102,41 @@
         def _():
             copy_x(e, yh, 1 - xh).wait_recv()
 
+    lane8 = lax.broadcasted_iota(jnp.int32, (TILE_Y, TILE_X), 1)
+    row8 = lax.broadcasted_iota(jnp.int32, (TILE_Y, TILE_X), 0)
+
+    def cut(yh, xh):
+        return pl.ds(yh * TILE_Y, TILE_Y), pl.ds(xh * TILE_X, TILE_X)
+
+    def pack_faces(e, yh, xh):
+        ys, xs = cut(yh, xh)
+        edge = yh * (rows - 1)
+        packed = [jnp.zeros((TILE_Y, TILE_X), F32) for _ in range(4)]
+        for index in range(planes * V):
+            z, v = divmod(index, V)
+            send_y[e, yh, xh, index] = pv[z, v, edge:edge + 1, xs]
+            turned = pltpu.roll(pv[z, v, ys, xs], index + 2 * xh, 1)
+            packed[index % 4] = jnp.where(lane8 == index + xh, turned, packed[index % 4])
+        send_x[e, xh, yh] = (packed[0] + packed[1]) + (packed[2] + packed[3])
+
+    def unrolled(step, carry, upward=True):
+        def turn(i, carry):
+            for j in range(PLANES_AT_ONCE):
+                at = i * PLANES_AT_ONCE + j
+                carry = step(at if upward else planes - 1 - at, carry)
+            return carry
+
+        return lax.fori_loop(0, planes // PLANES_AT_ONCE, turn, carry)
+
+    load_prev.wait()
+    for yh, xh in CHUNKS:
+        pack_faces(0, yh, xh)
+
+    pl.semaphore_wait(barrier, sum(exists.astype(jnp.int32) for _, _, exists in sides))
+
+    for yh, xh in CHUNKS:
+        start_faces(0, yh, xh)
+
     for side in range(2):
 
         @pl.when(jnp.logical_not(has_y[side]))
@@ -115,34 +151,13 @@
                 for yh in range(2):
                     recv_x[e, side, yh] = jnp.zeros(recv_x.shape[3:], F32)
 
-    lane8 = lax.broadcasted_iota(jnp.int32, (TILE_Y, TILE_X), 1)
-    row8 = lax.broadcasted_iota(jnp.int32, (TILE_Y, TILE_X), 0)
-
-    def cut(yh, xh):
-        return pl.ds(yh * TILE_Y, TILE_Y), pl.ds(xh * TILE_X, TILE_X)
-
-    def pack_faces(e, yh, xh, z, values, packed):
-        for v in range(V):
-            index = z * V + v
-            edge = (TILE_Y - 1) * yh
-            send_y[e, yh, xh, index] = values[v][edge:edge + 1, :]
-            packed = jnp.where(
-                lane8 == index, pltpu.roll(values[v], lax.rem(index + xh, TILE_X), 1), packed)
-        return packed
-
-    load_prev.wait()
-    for yh, xh in CHUNKS:
-        ys, xs = cut(yh, xh)
-
-        def pack(z, packed):
-            return pack_faces(0, yh, xh, z, [pv[z, v, ys, xs] for v in range(V)], packed)
-
-        send_x[0, xh, yh] = lax.fori_loop(0, planes, pack, jnp.zeros((TILE_Y, TILE_X), F32))
-
-    pl.semaphore_wait(barrier, sum(exists.astype(jnp.int32) for _, _, exists in sides))
-
-    for yh, xh in CHUNKS:
-        start_faces(0, yh, xh)
+    @pl.when(iz == 0)
+    def _():
+        recv_z[0] = jnp.zeros(recv_z.shape[1:], F32)
+
+    @pl.when(iz == nz - 1)
+    def _():
+        recv_z[1] = jnp.zeros(recv_z.shape[1:], F32)
 
     lane = lax.broadcasted_iota(jnp.int32, (rows, cols), 1)
     row = lax.broadcasted_iota(jnp.int32, (rows, cols), 0)
@@ -173,59 +188,66 @@
             out.append(((terms[0] + terms[1]) + (terms[2] + terms[3])) + (terms[4] + terms[5]))
         return out
 
-    def add_halo(e, yh, xh, sign):
+    def add_halo(e, yh, xh):
         ys, xs = cut(yh, xh)
         wait_faces(e, yh, xh)
         packed = recv_x[e, xh, yh]
         on_row = row8 == (TILE_Y - 1) * yh
         on_lane = lane8 == (TILE_X - 1) * xh
 
-        @pl.loop(0, planes)
-        def _(z):
+        def step(z, carry):
             hy, hx = [], []
             for v in range(V):
                 index = z * V + v
                 hy.append(jnp.where(on_row, recv_y[e, yh, xh, index], 0.0))
-                turn = lax.rem(TILE_X + (TILE_X - 1) * xh - index, TILE_X)
-                hx.append(jnp.where(on_lane, pltpu.roll(packed, turn, 1), 0.0))
+                hx.append(jnp.where(on_lane, pltpu.roll(packed, TILE_X - 1 - index, 1), 0.0))
             fx = matvec(lambda a, b: jv[z, xh, a, b, ys, xs], hx)
             fy = matvec(lambda a, b: jv[z, 2 + yh, a, b, ys, xs], hy)
             for a in range(V):
-                rv[z, a, ys, xs] = rv[z, a, ys, xs] + sign * (fx[a] + fy[a])
-
-    def sweep_up(c, incoming):
+                if e == 0:
+                    rv[z, a, ys, xs] = rv[z, a, ys, xs] - (fx[a] + fy[a])
+                else:
+                    rv[z, a, ys, xs] = rv[z, a, ys, xs] + (fx[a] + fy[a])
+            return carry
+
+        unrolled(step, 0)
+
+    def sweep_up(c):
         yh, xh = CHUNKS[c]
         ys, xs = cut(yh, xh)
 
-        def step(z, carry):
-            below, packed = carry
+        @pl.when(iz > 0)
+        def _():
+            copy_z(0, c).wait_recv()
+
+        def step(z, below):
             lower = matvec(lambda a, b: jv[z, 4, a, b, ys, xs], below)
             source = [rv[z, a, ys, xs] - lower[a] for a in range(V)]
             result = matvec(lambda a, b: dv[z, a, b, ys, xs], source)
-            change = []
             for a in range(V):
                 sv[z, a, ys, xs] = result[a]
-                change.append(result[a] - pv[z, a, ys, xs])
-                pv[z, a, ys, xs] = change[a]
-            return tuple(result), pack_faces(1, yh, xh, z, change, packed)
-
-        top, packed = lax.fori_loop(
-            0, planes, step, (tuple(incoming), jnp.zeros((TILE_Y, TILE_X), F32)))
+                pv[z, a, ys, xs] = result[a] - pv[z, a, ys, xs]
+            return tuple(result)
+
+        top = unrolled(step, tuple(recv_z[0, c, v] for v in range(V)))
         for v in range(V):
             send_z[0, c, v] = top[v]
-        send_x[1, xh, yh] = packed
 
         @pl.when(iz < nz - 1)
         def _():
             copy_z(0, c).start()
 
+        pack_faces(1, yh, xh)
         start_faces(1, yh, xh)
 
-    def sweep_down(c, incoming):
+    def sweep_down(c):
         ys, xs = cut(*CHUNKS[c])
 
-        def step(i, above):
-            z = planes - 1 - i
+        @pl.when(iz < nz - 1)
+        def _():
+            copy_z(1, c).wait_recv()
+
+        def step(z, above):
             upper = matvec(lambda a, b: jv[z, 5, a, b, ys, xs], above)
             change = [rv[z, a, ys, xs] + upper[a] for a in range(V)]
             change = matvec(lambda a, b: dv[z, a, b, ys, xs], change)
@@ -234,15 +256,13 @@
                 out_ref[z, a, ys, xs] = result[a]
             return tuple(result)
 
-        bottom = lax.fori_loop(0, planes, step, tuple(incoming))
+        bottom = unrolled(step, tuple(recv_z[1, c, v] for v in range(V)), upward=False)
         for v in range(V):
             send_z[1, c, v] = bottom[v]
 
         @pl.when(iz > 0)
         def _():
             copy_z(1, c).start()
-
-    zeros = [jnp.zeros((TILE_Y, TILE_X), F32)] * V
 
     @pl.loop(0, planes)
     def _(z):
@@ -256,17 +276,8 @@
             copy.wait()
 
     for c, (yh, xh) in enumerate(CHUNKS):
-        add_halo(0, yh, xh, -1.0)
-
-        @pl.when(iz == 0)
-        def _():
-            sweep_up(c, zeros)
-
-    @pl.when(iz > 0)
-    def _():
-        for c in range(len(CHUNKS)):
-            copy_z(0, c).wait_recv()
-            sweep_up(c, [recv_z[0, c, v] for v in range(V)])
+        add_halo(0, yh, xh)
+        sweep_up(c)
 
     @pl.loop(0, planes)
     def _(z):
@@ -278,17 +289,8 @@
             copy.wait()
 
     for c, (yh, xh) in enumerate(CHUNKS):
-        add_halo(1, yh, xh, 1.0)
-
-        @pl.when(iz == nz - 1)
-        def _():
-            sweep_down(c, zeros)
-
-    @pl.when(iz < nz - 1)
-    def _():
-        for c in range(len(CHUNKS)):
-            copy_z(1, c).wait_recv()
-            sweep_down(c, [recv_z[1, c, v] for v in range(V)])
+        add_halo(1, yh, xh)
+        sweep_down(c)
 
     for e in range(2):
         for yh, xh in CHUNKS:
@@ -320,7 +322,7 @@
     planes, _, rows, cols = rhs.shape
     faces = planes * V
     n = len(CHUNKS)
-    hbm = pl.BlockSpec(memory_space=pl.ANY)
+    hbm = pl.BlockSpec(memory_space=pltpu.HBM)
     dma = pltpu.SemaphoreType.DMA
     out = pl.pallas_call(
         functools.partial(kernel, sizes),
@@ -344,9 +346,9 @@
             dma((2, n)), dma((2, n)),
         ],
         compiler_params=pltpu.CompilerParams(
-            collective_id=0, has_side_effects=True, vmem_limit_bytes=60 * 1024 * 1024),
+            collective_id=0, has_side_effects=True, vmem_limit_bytes=30 * 1024 * 1024),
         name="sweep_pair",
-    )(rhs, prev, dinv, jac)
+    )(*(pltpu.with_memory_space_constraint(x, pltpu.HBM) for x in (rhs, prev, dinv, jac)))
     return jnp.transpose(out, (0, 2, 1, 3))
 
 

time: 50 us -> 37.5 us (0.75)
  Pallas kernels: 47.6 us -> 36.5 us
  local copies, waits for them, and re-layouts: 2.21 us -> 0.95 us
    pallas_call x1, Pallas kernels: 47.6 us -> 36.5 us  [body(): pl.pallas_call(functools.partial(kernel, sizes), out_shape=jax.ShapeDtype...]
    unnamed x1, local copies, waits for them, and re-layouts: 2.21 us -> 0.95 us
where the time goes in v2:
time: 37.5 us; the launch traced here: 37.4 us
  Pallas kernels  36.5 us (97%)
  local copies, waits for them, and re-layouts  0.95 us (3%)
    pallas_call x1, Pallas kernels, body(): pl.pallas_call(functools.partial(kernel, sizes), out_shape=jax.ShapeDtype...  36.5 us
    unnamed x1, local copies, waits for them, and re-layouts  0.95 us

profile of v2, /device:TPU:6, one launch (start us, length us, event | category | flops | bytes accessed | tf_op | source)
XLA Modules:
  0.0 37.4 jit_solution(10679009359087997591)
XLA Ops:
  0.0 36.5 %sweep_pair.1 = f32[10,6,16,256]{3,2,1,0:T(8,128)S(1)} custom-call(f32[10,6,16,256]{3,2,1,0:T(8,128)} %bitcast.8, f32[10,6,16,256]{3,2,1,0:T(8,128)} %bitcast.9, bf16[10,6,6,16,256]{4,3,2,1,0:T(8,128)(2,1)} %bitcast.7, bf16[10,6,6,6,16,256]{5,4,3,2,1,0:T(8,128)(2,1)} %bitcast.6), custom_call_target="tpu_custom_call" | custom-call | tf_op jit(solution)/shard_map/sweep_pair/pallas_call | solution.py:327
  36.5 0.9 %copy.6 = f32[10,16,6,256]{3,1,2,0:T(8,128)} copy(f32[10,16,6,256]{3,1,2,0:T(8,128)S(1)} %bitcast.5) | data formatting | bytes 1966080

commit v3 on v2

--- a/solution.py
+++ b/solution.py
@@ -14,9 +14,9 @@
 CHUNKS = ((0, 0), (1, 0), (0, 1), (1, 1))
 
 
-def kernel(sizes, rhs_h, prev_h, dinv_h, jac_h, out_ref, jv, dv, rv, pv, sv,
+def kernel(sizes, rhs_h, prev_h, dinv_h, jac_h, out_ref, jv, dv, mv, rv, pv, sv,
            send_y, recv_y, send_x, recv_x, send_z, recv_z,
-           ld_p, ld_r, ld_j, ld_l, ld_d, ld_u, ssy, rsy, ssx, rsx, ssz, rsz):
+           ld_p, ld_r, ld_j, ld_l, ld_u, ssy, rsy, ssx, rsx, ssz, rsz):
     nz, nx, ny = sizes
     planes, _, rows, cols = rhs_h.shape
     iz, ix, iy = (lax.axis_index(a) for a in ("gz", "gx", "gy"))
@@ -25,27 +25,26 @@
     load_prev.start()
 
     def load_first(z):
+        return pltpu.make_async_copy(
+            jac_h.at[z, pl.ds(0, 4)], jv.at[z, pl.ds(0, 4)], ld_j.at[z])
+
+    @pl.loop(0, planes)
+    def _(z):
+        load_first(z).start()
+
+
+    load_rhs = pltpu.make_async_copy(rhs_h, sv, ld_r)
+
+    def load_lower(xh):
+        xs = pl.ds(xh * TILE_X, TILE_X)
         return (
-            pltpu.make_async_copy(jac_h.at[z, pl.ds(0, 4)], jv.at[z, pl.ds(0, 4)], ld_j.at[z]),
-            pltpu.make_async_copy(rhs_h.at[z], rv.at[z], ld_r.at[z]),
+            pltpu.make_async_copy(
+                jac_h.at[:, 4, :, :, :, xs], jv.at[:, 4, :, :, :, xs], ld_l.at[xh, 0]),
+            pltpu.make_async_copy(
+                dinv_h.at[:, :, :, :, xs], dv.at[:, :, :, :, xs], ld_l.at[xh, 1]),
         )
 
-    def load_lower(z):
-        return (
-            pltpu.make_async_copy(jac_h.at[z, 4], jv.at[z, 4], ld_l.at[z]),
-            pltpu.make_async_copy(dinv_h.at[z], dv.at[z], ld_d.at[z]),
-        )
-
-    def load_upper(z):
-        return (pltpu.make_async_copy(jac_h.at[z, 5], jv.at[z, 5], ld_u.at[z]),)
-
-    for group in (load_first, load_lower, load_upper):
-
-        @pl.loop(0, planes)
-        def _(z):
-            for copy in group(z):
-                copy.start()
-
+    load_upper = pltpu.make_async_copy(jac_h.at[:, 5], jv.at[:, 5], ld_u)
     sides = (
         ("gy", -1, iy > 0), ("gy", 1, iy < ny - 1),
         ("gx", -1, ix > 0), ("gx", 1, ix < nx - 1),
@@ -129,6 +128,9 @@
         return lax.fori_loop(0, planes // PLANES_AT_ONCE, turn, carry)
 
     load_prev.wait()
+    for copy in (load_rhs,) + load_lower(0):
+        copy.start()
+
     for yh, xh in CHUNKS:
         pack_faces(0, yh, xh)
 
@@ -166,7 +168,7 @@
         (row == 0, 1, 0), (row == rows - 1, rows - 1, 0),
     )
 
-    def interior(z, subtract):
+    def interior(z):
         f = [pv[z, v] for v in range(V)]
         for n, (edge, shift, axis) in enumerate(shifts):
             g = [jnp.where(edge, 0.0, pltpu.roll(x, shift, axis)) for x in f]
@@ -174,9 +176,7 @@
                 total = jv[z, n, a, 0].astype(F32) * g[0]
                 for b in range(1, V):
                     total = total + jv[z, n, a, b].astype(F32) * g[b]
-                if subtract:
-                    rv[z, a] = rv[z, a] - total
-                elif n == 0:
+                if n == 0:
                     rv[z, a] = total
                 else:
                     rv[z, a] = rv[z, a] + total
@@ -205,7 +205,7 @@
             fy = matvec(lambda a, b: jv[z, 2 + yh, a, b, ys, xs], hy)
             for a in range(V):
                 if e == 0:
-                    rv[z, a, ys, xs] = rv[z, a, ys, xs] - (fx[a] + fy[a])
+                    rv[z, a, ys, xs] = sv[z, a, ys, xs] - (rv[z, a, ys, xs] + (fx[a] + fy[a]))
                 else:
                     rv[z, a, ys, xs] = rv[z, a, ys, xs] + (fx[a] + fy[a])
             return carry
@@ -237,15 +237,22 @@
         def _():
             copy_z(0, c).start()
 
-        pack_faces(1, yh, xh)
-        start_faces(1, yh, xh)
+        @pl.when(iz == nz - 1)
+        def _():
+            pack_faces(1, yh, xh)
+            start_faces(1, yh, xh)
+
+    def finish_down(c, step):
+        bottom = unrolled(step, tuple(recv_z[1, c, v] for v in range(V)), upward=False)
+        for v in range(V):
+            send_z[1, c, v] = bottom[v]
+
+        @pl.when(iz > 0)
+        def _():
+            copy_z(1, c).start()
 
     def sweep_down(c):
         ys, xs = cut(*CHUNKS[c])
-
-        @pl.when(iz < nz - 1)
-        def _():
-            copy_z(1, c).wait_recv()
 
         def step(z, above):
             upper = matvec(lambda a, b: jv[z, 5, a, b, ys, xs], above)
@@ -256,41 +263,80 @@
                 out_ref[z, a, ys, xs] = result[a]
             return tuple(result)
 
-        bottom = unrolled(step, tuple(recv_z[1, c, v] for v in range(V)), upward=False)
-        for v in range(V):
-            send_z[1, c, v] = bottom[v]
-
-        @pl.when(iz > 0)
-        def _():
-            copy_z(1, c).start()
+        finish_down(c, step)
+
+    def fold(c):
+        ys, xs = cut(*CHUNKS[c])
+
+        @pl.loop(0, planes)
+        def _(z):
+            inner = [rv[z, b, ys, xs] for b in range(V)]
+            upper = [[jv[z, 5, k, b, ys, xs].astype(F32) for b in range(V)] for k in range(V)]
+            for a in range(V):
+                inverse = [dv[z, a, k, ys, xs].astype(F32) for k in range(V)]
+                for b in range(V):
+                    terms = [inverse[k] * upper[k][b] for k in range(V)]
+                    mv[z, a, b, ys, xs] = (
+                        ((terms[0] + terms[1]) + (terms[2] + terms[3])) + (terms[4] + terms[5]))
+                terms = [inverse[k] * inner[k] for k in range(V)]
+                sv[z, a, ys, xs] = sv[z, a, ys, xs] - (
+                    ((terms[0] + terms[1]) + (terms[2] + terms[3])) + (terms[4] + terms[5]))
+
+    def sweep_down_folded(c):
+        ys, xs = cut(*CHUNKS[c])
+        copy_z(1, c).wait_recv()
+
+        def step(z, above):
+            change = matvec(lambda a, b: mv[z, a, b, ys, xs], above)
+            result = [sv[z, a, ys, xs] - change[a] for a in range(V)]
+            for a in range(V):
+                out_ref[z, a, ys, xs] = result[a]
+            return tuple(result)
+
+        finish_down(c, step)
 
     @pl.loop(0, planes)
     def _(z):
-        for copy in load_first(z):
-            copy.wait()
-        interior(z, True)
+        load_first(z).wait()
+        interior(z)
+
+    for copy in load_lower(1) + (load_upper,):
+        copy.start()
+
+    for c, (yh, xh) in enumerate(CHUNKS):
+        if c == 0:
+            load_rhs.wait()
+        if yh == 0:
+            for copy in load_lower(xh):
+                copy.wait()
+        add_halo(0, yh, xh)
+        sweep_up(c)
+
+    @pl.when(iz < nz - 1)
+    def _():
+        for yh, xh in CHUNKS:
+            pack_faces(1, yh, xh)
+            start_faces(1, yh, xh)
 
     @pl.loop(0, planes)
     def _(z):
-        for copy in load_lower(z):
-            copy.wait()
-
-    for c, (yh, xh) in enumerate(CHUNKS):
-        add_halo(0, yh, xh)
-        sweep_up(c)
-
-    @pl.loop(0, planes)
-    def _(z):
-        interior(z, False)
-
-    @pl.loop(0, planes)
-    def _(z):
-        for copy in load_upper(z):
-            copy.wait()
-
-    for c, (yh, xh) in enumerate(CHUNKS):
-        add_halo(1, yh, xh)
-        sweep_down(c)
+        interior(z)
+
+    load_upper.wait()
+
+    @pl.when(iz == nz - 1)
+    def _():
+        for c, (yh, xh) in enumerate(CHUNKS):
+            add_halo(1, yh, xh)
+            sweep_down(c)
+
+    @pl.when(iz < nz - 1)
+    def _():
+        for c, (yh, xh) in enumerate(CHUNKS):
+            add_halo(1, yh, xh)
+            fold(c)
+        for c in range(len(CHUNKS)):
+            sweep_down_folded(c)
 
     for e in range(2):
         for yh, xh in CHUNKS:
@@ -332,6 +378,7 @@
         scratch_shapes=[
             pltpu.VMEM(jac.shape, jac.dtype),
             pltpu.VMEM(dinv.shape, dinv.dtype),
+            pltpu.VMEM(dinv.shape, F32),
             pltpu.VMEM(rhs.shape, F32),
             pltpu.VMEM(rhs.shape, F32),
             pltpu.VMEM(rhs.shape, F32),
@@ -341,12 +388,12 @@
             pltpu.VMEM((2, 2, 2, TILE_Y, TILE_X), F32),
             pltpu.VMEM((2, n, V, TILE_Y, TILE_X), F32),
             pltpu.VMEM((2, n, V, TILE_Y, TILE_X), F32),
-            dma, dma((planes,)), dma((planes,)), dma((planes,)), dma((planes,)), dma((planes,)),
+            dma, dma, dma((planes,)), dma((2, 2)), dma,
             dma((2, 2, 2)), dma((2, 2, 2)), dma((2, 2, 2)), dma((2, 2, 2)),
             dma((2, n)), dma((2, n)),
         ],
         compiler_params=pltpu.CompilerParams(
-            collective_id=0, has_side_effects=True, vmem_limit_bytes=30 * 1024 * 1024),
+            collective_id=0, has_side_effects=True, vmem_limit_bytes=40 * 1024 * 1024),
         name="sweep_pair",
     )(*(pltpu.with_memory_space_constraint(x, pltpu.HBM) for x in (rhs, prev, dinv, jac)))
     return jnp.transpose(out, (0, 2, 1, 3))

time: 37.5 us -> 36.6 us (0.976)
  Pallas kernels: 36.5 us -> 35.6 us
    pallas_call x1, Pallas kernels: 36.5 us -> 35.6 us  [body(): pl.pallas_call(functools.partial(kernel, sizes), out_shape=jax.ShapeDtype...]
where the time goes in v3:
time: 36.6 us; the launch traced here: 36.5 us
  Pallas kernels  35.6 us (97%)
  local copies, waits for them, and re-layouts  0.95 us (3%)
    pallas_call x1, Pallas kernels, body(): pl.pallas_call(functools.partial(kernel, sizes), out_shape=jax.ShapeDtype...  35.6 us
    unnamed x1, local copies, waits for them, and re-layouts  0.95 us

profile of v3, /device:TPU:6, one launch (start us, length us, event | category | flops | bytes accessed | tf_op | source)
XLA Modules:
  0.0 36.5 jit_solution(11840931946249425553)
XLA Ops:
  0.0 35.6 %sweep_pair.1 = f32[10,6,16,256]{3,2,1,0:T(8,128)S(1)} custom-call(f32[10,6,16,256]{3,2,1,0:T(8,128)} %bitcast.8, f32[10,6,16,256]{3,2,1,0:T(8,128)} %bitcast.9, bf16[10,6,6,16,256]{4,3,2,1,0:T(8,128)(2,1)} %bitcast.7, bf16[10,6,6,6,16,256]{5,4,3,2,1,0:T(8,128)(2,1)} %bitcast.6), custom_call_target="tpu_custom_call" | custom-call | tf_op jit(solution)/shard_map/sweep_pair/pallas_call | solution.py:373
  35.6 0.9 %copy.6 = f32[10,16,6,256]{3,1,2,0:T(8,128)} copy(f32[10,16,6,256]{3,1,2,0:T(8,128)S(1)} %bitcast.5) | data formatting | bytes 1966080

commit v4 on v3

--- a/solution.py
+++ b/solution.py
@@ -10,7 +10,7 @@
 F32 = jnp.float32
 V = 6
 TILE_Y, TILE_X = 8, 128
-PLANES_AT_ONCE = 5
+PLANES_AT_ONCE = 10
 CHUNKS = ((0, 0), (1, 0), (0, 1), (1, 1))
 
 
@@ -84,13 +84,13 @@
     has_x = (ix > 0, ix < nx - 1)
 
     def start_faces(e, yh, xh):
+        @pl.when(has_x[xh])
+        def _():
+            copy_x(e, yh, xh).start()
+
         @pl.when(has_y[yh])
         def _():
             copy_y(e, yh, xh).start()
-
-        @pl.when(has_x[xh])
-        def _():
-            copy_x(e, yh, xh).start()
 
     def wait_faces(e, yh, xh):
         @pl.when(has_y[yh])

time: 36.6 us -> 36.1 us (0.986)
  Pallas kernels: 35.6 us -> 35 us
    pallas_call x1, Pallas kernels: 35.6 us -> 35 us  [body(): pl.pallas_call(functools.partial(kernel, sizes), out_shape=jax.ShapeDtype...]
where the time goes in v4:
time: 36.1 us; the launch traced here: 36 us
  Pallas kernels  35 us (97%)
  local copies, waits for them, and re-layouts  0.95 us (3%)
    pallas_call x1, Pallas kernels, body(): pl.pallas_call(functools.partial(kernel, sizes), out_shape=jax.ShapeDtype...  35 us
    unnamed x1, local copies, waits for them, and re-layouts  0.95 us

profile of v4, /device:TPU:6, one launch (start us, length us, event | category | flops | bytes accessed | tf_op | source)
XLA Modules:
  0.0 36.0 jit_solution(555555300255068163)
XLA Ops:
  0.0 35.0 %sweep_pair.1 = f32[10,6,16,256]{3,2,1,0:T(8,128)S(1)} custom-call(f32[10,6,16,256]{3,2,1,0:T(8,128)} %bitcast.8, f32[10,6,16,256]{3,2,1,0:T(8,128)} %bitcast.9, bf16[10,6,6,16,256]{4,3,2,1,0:T(8,128)(2,1)} %bitcast.7, bf16[10,6,6,6,16,256]{5,4,3,2,1,0:T(8,128)(2,1)} %bitcast.6), custom_call_target="tpu_custom_call" | custom-call | tf_op jit(solution)/shard_map/sweep_pair/pallas_call | solution.py:373
  35.0 0.9 %copy.6 = f32[10,16,6,256]{3,1,2,0:T(8,128)} copy(f32[10,16,6,256]{3,1,2,0:T(8,128)S(1)} %bitcast.5) | data formatting | bytes 1966080
